TPU v7x, 32 devices: a whole 2x2x4 slice. The times are simulated.
32 devices in a mesh: seq: 8 (over z, x), hid: 4 (over y, core).
Axes of the slice: x: 2, y: 2, z: 4, core: 2. Of those that a mesh axis runs over, the one named last changes fastest.
Arguments:
- tokens: bfloat16 [1024, 4096], P('seq', 'hid'), may hold values from -6 to 6
- hidden_grad: bfloat16 [1024, 14336], P('seq', 'hid'), may hold values from -6 to 6
- gate_blocks: bfloat16 [4, 448, 128, 128], P('hid', 'seq'), may hold values from -0.125 to 0.125
- up_blocks: bfloat16 [4, 448, 128, 128], P('hid', 'seq'), may hold values from -0.125 to 0.125
- gate_rows: int32 [4, 448], P('hid'), may hold values from 0 to 31, as said below
- gate_cols: int32 [4, 448], P('hid'), may hold values from 0 to 27
- gate_count: int32 [4], P('hid'), may hold values from 56 to 448, as said below
- up_rows: int32 [4, 448], P('hid'), may hold values from 0 to 31, as said below
- up_cols: int32 [4, 448], P('hid'), may hold values from 0 to 27
- up_count: int32 [4], P('hid'), may hold values from 56 to 448, as said below
Outputs:
- hidden: bfloat16 [1024, 14336], P('seq', 'hid')
- input_grad: bfloat16 [1024, 4096], P('seq', 'hid')
- gate_block_grads: bfloat16 [4, 448, 128, 128], P('hid', 'seq')
- up_block_grads: bfloat16 [4, 448, 128, 128], P('hid', 'seq')
Inputs may be any that keep to these rules, and one draw needn't show every extreme that they name: For each panel, the pairs (gate_rows, gate_cols) over all 448 slots are distinct. `gate_count`: slots at or after a panel's count hold no block of the matrix. For each panel, the pairs (up_rows, up_cols) over all 448 slots are distinct. `up_count`: slots at or after a panel's count hold no block of the matrix.
All inputs are finite; a program needn't handle non-finite values.
Results may differ from a plain program's by a relative error of at most 0.018.
Values may be sent and summed in bfloat16 or wider, within the bound.
A program may use at most 192 MiB of HBM per device.

v0:
```python
import math
import jax
import jax.numpy as jnp
from jax import lax
from jax.sharding import PartitionSpec as P


def swapped(value, axis, stride):
    mask = 2**stride
    pairs = [(source, source ^ mask) for source in range(lax.axis_size(axis))]
    return lax.ppermute(value, axis, pairs)


def silu_parts(preact):
    sigma = jax.nn.sigmoid(preact)
    return (preact * sigma, sigma * (1.0 + preact * (1.0 - sigma)))


def place_split(products, placing, form):
    high_part = products.astype(jnp.bfloat16)
    rest_part = (products - high_part.astype(jnp.float32)).astype(jnp.bfloat16)
    table = placing.astype(jnp.bfloat16)
    placed = jnp.einsum(form, high_part, table, preferred_element_type=jnp.float32)
    return placed + jnp.einsum(form, rest_part, table, preferred_element_type=jnp.float32)


def project_slots(tiles, weights, rows, columns, live_count, group_size, trips, col_blocks):
    tok_rows = tiles.shape[0]
    block_size = tiles.shape[2]
    targets = jnp.arange(col_blocks)
    offsets = jnp.arange(group_size)

    def project_one_group(group_index, running):
        start = group_index * group_size
        chosen = lax.dynamic_slice_in_dim(weights, start, group_size, 0)
        row_ids = lax.dynamic_slice_in_dim(rows, start, group_size, 0)
        col_ids = lax.dynamic_slice_in_dim(columns, start, group_size, 0)
        active = start + offsets < live_count
        picked = jnp.take(tiles, row_ids, axis=1)
        products = jnp.einsum("tsk,skn->tsn", picked, chosen, preferred_element_type=jnp.float32)
        placing = (col_ids[:, None] == targets[None, :]) & active[:, None]
        return running + place_split(products, placing, "tsn,sc->tcn")

    initial = jnp.zeros((tok_rows, col_blocks, block_size), jnp.float32)
    return lax.fori_loop(0, trips, project_one_group, initial)


def return_slots(grad_tiles, weights, rows, columns, live_count, group_size, trips, row_blocks):
    tok_rows = grad_tiles.shape[0]
    block_size = grad_tiles.shape[2]
    targets = jnp.arange(row_blocks)
    offsets = jnp.arange(group_size)

    def return_one_group(group_index, running):
        start = group_index * group_size
        chosen = lax.dynamic_slice_in_dim(weights, start, group_size, 0)
        row_ids = lax.dynamic_slice_in_dim(rows, start, group_size, 0)
        col_ids = lax.dynamic_slice_in_dim(columns, start, group_size, 0)
        active = start + offsets < live_count
        picked = jnp.take(grad_tiles, col_ids, axis=1)
        products = jnp.einsum("tsn,skn->tsk", picked, chosen, preferred_element_type=jnp.float32)
        placing = (row_ids[:, None] == targets[None, :]) & active[:, None]
        return running + place_split(products, placing, "tsk,sr->trk")

    initial = jnp.zeros((tok_rows, row_blocks, block_size), jnp.float32)
    return lax.fori_loop(0, trips, return_one_group, initial)


def on_device(
    tokens,
    hidden_grad,
    gate_blocks,
    up_blocks,
    gate_rows,
    gate_cols,
    gate_count,
    up_rows,
    up_cols,
    up_count,
):
    gathered = lax.all_gather(tokens, "hid", axis=1, tiled=True)
    tok_rows = gathered.shape[0]
    block_size = gate_blocks.shape[2]
    row_blocks = gathered.shape[1] // block_size
    col_blocks = hidden_grad.shape[1] // block_size
    gate_all = lax.all_gather(gate_blocks, "seq", axis=1, tiled=True)
    up_all = lax.all_gather(up_blocks, "seq", axis=1, tiled=True)
    capacity = gate_all.shape[1]
    group_size = 32
    groups = capacity // group_size
    gate_live = gate_count[0]
    up_live = up_count[0]
    tiles = gathered.reshape(tok_rows, row_blocks, block_size)
    gate_pre = project_slots(
        tiles, gate_all[0], gate_rows[0], gate_cols[0], gate_live, group_size, groups, col_blocks
    )
    up_pre = project_slots(
        tiles, up_all[0], up_rows[0], up_cols[0], up_live, group_size, groups, col_blocks
    )
    activated, slope = silu_parts(gate_pre)
    hidden = (activated * up_pre).astype(jnp.bfloat16)
    upstream = hidden_grad.reshape(tok_rows, col_blocks, block_size).astype(jnp.float32)
    gate_grad = (upstream * up_pre * slope).astype(jnp.bfloat16)
    up_grad = (upstream * activated).astype(jnp.bfloat16)
    input_sum = return_slots(
        gate_grad,
        gate_all[0],
        gate_rows[0],
        gate_cols[0],
        gate_live,
        group_size,
        groups,
        row_blocks,
    )
    input_sum = input_sum + return_slots(
        up_grad, up_all[0], up_rows[0], up_cols[0], up_live, group_size, groups, row_blocks
    )
    input_grad = lax.psum_scatter(
        input_sum.reshape(tok_rows, row_blocks * block_size).astype(jnp.bfloat16),
        "hid",
        scatter_dimension=1,
        tiled=True,
    )
    seq_count = lax.axis_size("seq")
    position = lax.axis_index("seq")
    levels = seq_count.bit_length() - 1
    blk_dev = capacity // seq_count
    other_tiles, other_gate, other_up = swapped((tiles, gate_grad, up_grad), "seq", 0)
    both_tiles = jnp.concatenate([tiles, other_tiles], axis=0)
    both_gate = jnp.concatenate([gate_grad, other_gate], axis=0)
    both_up = jnp.concatenate([up_grad, other_up], axis=0)
    parity = position % 2
    owners = 2 * jnp.arange(seq_count // 2) + parity
    slot_ids = (owners[:, None] * blk_dev + jnp.arange(blk_dev)[None, :]).reshape(-1)
    stacked = []
    for rows, columns, live_count, grad_tiles in (
        (gate_rows[0], gate_cols[0], gate_live, both_gate),
        (up_rows[0], up_cols[0], up_live, both_up),
    ):
        row_ids = jnp.take(rows, slot_ids)
        col_ids = jnp.take(columns, slot_ids)
        picked_input = jnp.take(both_tiles, row_ids, axis=1)
        picked_grad = jnp.take(grad_tiles, col_ids, axis=1)
        block_term = jnp.einsum(
            "tsk,tsn->skn", picked_input, picked_grad, preferred_element_type=jnp.float32
        )
        stacked.append(block_term * (slot_ids < live_count).astype(jnp.float32)[:, None, None])
    current = jnp.stack(stacked, axis=1)
    current = current.reshape((seq_count // 2, blk_dev) + current.shape[1:])
    for level in range(1, levels):
        own_bit = position // 2**level % 2
        halves = current.reshape((current.shape[0] // 2, 2) + current.shape[1:])
        kept = lax.dynamic_index_in_dim(halves, own_bit, 1, keepdims=False)
        sent = lax.dynamic_index_in_dim(halves, 1 - own_bit, 1, keepdims=False)
        received = swapped(sent.astype(jnp.bfloat16), "seq", level)
        current = kept + received.astype(jnp.float32)
    summed = current[0]
    scale = 1.0 / math.sqrt(tok_rows * seq_count)
    gate_block_grads = (summed[:, 0] * scale).astype(jnp.bfloat16)[None]
    up_block_grads = (summed[:, 1] * scale).astype(jnp.bfloat16)[None]
    return (
        hidden.reshape(tok_rows, col_blocks * block_size),
        input_grad,
        gate_block_grads,
        up_block_grads,
    )


def solution(mesh):
    placed = (
        P("seq", "hid"),
        P("seq", "hid"),
        P("hid", "seq", None, None),
        P("hid", "seq", None, None),
        P("hid", None),
        P("hid", None),
        P("hid"),
        P("hid", None),
        P("hid", None),
        P("hid"),
    )
    return jax.shard_map(
        on_device,
        mesh=mesh,
        in_specs=placed,
        out_specs=(
            P("seq", "hid"),
            P("seq", "hid"),
            P("hid", "seq", None, None),
            P("hid", "seq", None, None),
        ),
        check_vma=False,
    )
```

profile of v0, /device:TPU:0, one launch (start us, length us, event | category | flops | bytes accessed | tf_op | source)
XLA Modules:
  0.0 1165.3 jit_solution(1844786483724718215)
XLA Ops:
  16.3 13.3 %all-gather.6.cloned.1.call-done = bf16[128,4096]{0,1:T(8,128)(2,1)} async-done(((bf16[128,1024]{0,1:T(8,128)(2,1)}), bf16[128,4096]{0,1:T(8,128)(2,1)}) %all-gather.6.cloned.1.call-update) | async-done | bytes 1048592 | tf_op jit(solution)/shard_map/all_gather | solution.py:81
  33.3 200.2 %all-gather.8.cloned.1.call-done = bf16[1,448,128,128]{3,2,0,1:T(8,128)(2,1)} async-done(((bf16[1,56,128,128]{3,2,0,1:T(8,128)(2,1)}), bf16[1,448,128,128]{3,2,0,1:T(8,128)(2,1)}) %all-gather.8.cloned.1.call-update) | async-done | bytes 14680080 | tf_op jit(solution)/shard_map/all_gather | solution.py:87
  233.5 192.3 %while.61 = (s32[]{:T(128)}, f32[128,28,128]{2,1,0:T(8,128)}, s32[448]{0:T(512)S(1)}, s32[]{:T(128)}, bf16[448,128,128]{2,1,0:T(8,128)(2,1)}, /*index=5*/s32[448...) while((s32[]{:T(128)}, f32[128,28,128]{2,1,0:T(8,128)}, ...), condition=%wide.region_3.5_spmd.clone, body=%wide.region_2.4_spmd.clone.sunk | while | flops 196940544 | bytes 19928416 | solution.py:45
  311.5 4.6 bitcast_add_fusion.9
  425.8 9.8 all-gather.4.cloned.1.call-done
  435.6 193.2 %while.60 = (s32[]{:T(128)}, f32[128,28,128]{2,1,0:T(8,128)}, s32[448]{0:T(512)S(1)}, s32[]{:T(128)}, bf16[448,128,128]{2,1,0:T(8,128)(2,1)}, /*index=5*/s32[448...) while((s32[]{:T(128)}, f32[128,28,128]{2,1,0:T(8,128)}, ...), condition=%wide.region_1.3_spmd.clone, body=%wide.region_0.2_spmd.clone.sunk | while | flops 196940544 | bytes 19928416 | solution.py:45
  628.8 6.5 multiply_convert_fusion.1
  645.1 9.4 gather_fusion.5
  654.5 9.2 gather_fusion.9
  665.3 9.2 gather_fusion.7
  678.0 9.1 gather_fusion.11
  687.2 18.4 %fusion.105 = f32[224,128,128]{2,1,0:T(8,128)} fusion(bf16[224,256,128]{2,1,0:T(8,128)(2,1)} %gather_fusion.7, pred[224]{0:T(512)(128)(4,1)S(1)} %get-tuple-element.961, bf16[224,256,128]{2,1,0:T(8,128)(2,1)} %gather_fusion.5, pred[224]{0:T(512)(128)(4,1)S(1)} %get-tuple-element.963, f32[224]{0:T(256)S(1)} %get-tuple-element.960), kind=kOutput, calls=%fused_computation.141 | convolution fusion | flops 1897398272 | bytes 44041536 | tf_op jit(solution)/shard_map/tsk,tsn->skn/dot_general | solution.py:144
  705.6 18.5 %fusion.110 = f32[224,128,128]{2,1,0:T(8,128)} fusion(bf16[224,256,128]{2,1,0:T(8,128)(2,1)} %gather_fusion.11, pred[224]{0:T(512)(128)(4,1)S(1)} %get-tuple-element.944, bf16[224,256,128]{2,1,0:T(8,128)(2,1)} %gather_fusion.9, pred[224]{0:T(512)(128)(4,1)S(1)} %get-tuple-element.941, f32[224]{0:T(256)S(1)} %get-tuple-element.959), kind=kOutput, calls=%fused_computation.142 | convolution fusion | flops 1897398272 | bytes 44041536 | tf_op jit(solution)/shard_map/tsk,tsn->skn/dot_general | solution.py:144
  724.1 10.1 fusion.115
  734.2 192.1 %while.62 = (s32[]{:T(128)}, f32[128,32,128]{2,1,0:T(8,128)}, s32[448]{0:T(512)S(1)}, s32[]{:T(128)}, bf16[448,128,128]{2,1,0:T(8,128)(2,1)}, /*index=5*/s32[448...) while((s32[]{:T(128)}, f32[128,32,128]{2,1,0:T(8,128)}, ...), condition=%wide.region_5.8_spmd.clone.clone, body=%wide.region_4.0_spmd.clone.clone.sunk | while | flops 205526272 | bytes 20976992 | solution.py:66
  926.2 8.6 fusion.90
  934.9 5.1 copy-done.7
  945.5 186.0 %while.63 = (s32[]{:T(128)}, f32[128,32,128]{2,1,0:T(8,128)}, s32[448]{0:T(512)}, s32[]{:T(128)}, bf16[448,128,128]{2,1,0:T(8,128)(2,1)}, /*index=5*/s32[448]{0:...) while((s32[]{:T(128)}, f32[128,32,128]{2,1,0:T(8,128)}, ...), condition=%wide.region_7.10_spmd.clone.clone, body=%wide.region_6.9_spmd.clone.clone.sunk | while | flops 205526272 | bytes 24647044 | solution.py:66
  967.5 3.9 bitcast_add_fusion.11
  980.9 3.9 bitcast_add_fusion.11
  994.2 3.9 bitcast_add_fusion.11
  1007.5 3.9 bitcast_add_fusion.11
  1020.9 3.9 bitcast_add_fusion.11
  1034.2 3.9 bitcast_add_fusion.11
  1047.5 3.9 bitcast_add_fusion.11
  1060.8 3.9 bitcast_add_fusion.11
  1074.2 3.9 bitcast_add_fusion.11
  1087.5 3.9 bitcast_add_fusion.11
  1100.8 3.9 bitcast_add_fusion.11
  1127.5 3.9 bitcast_add_fusion.11
  1137.6 5.8 add_bitcast_fusion
  1146.2 12.6 %reduce-scatter.2.cloned.1.call-done = bf16[128,1024]{1,0:T(8,128)(2,1)} async-done(((bf16[128,4096]{1,0:T(8,128)(2,1)}), bf16[128,1024]{1,0:T(8,128)(2,1)}) %reduce-scatter.2.cloned.1.call-update) | async-done | bytes 262160 | tf_op jit(solution)/shard_map/reduce_scatter | solution.py:118
  (585 shorter events, 751.0 us)
Async XLA Ops:
  7.2 22.4 %all-gather.6.cloned.1.call-start = ((), (), s32[]{:S(2)}) async-start(), calls=%async_computation.2 | async-start | bytes 1310720 | tf_op jit(solution)/shard_map/all_gather | solution.py:81
  9.0 1.6 copy-start.9
  9.0 224.4 %all-gather.8.cloned.1.call-start = ((), (), s32[]{:S(2)}) async-start(), calls=%async_computation.3 | async-start | bytes 16515072 | tf_op jit(solution)/shard_map/all_gather | solution.py:87
  9.8 425.8 %all-gather.4.cloned.1.call-start = ((), (), s32[]{:S(2)}) async-start(), calls=%async_computation.1 | async-start | bytes 16515072 | tf_op jit(solution)/shard_map/all_gather | solution.py:86
  10.5 1148.3 %reduce-scatter.2.cloned.1.call-start = ((), (), s32[]{:S(2)}) async-start(), calls=%async_computation.4 | async-start | bytes 1310720 | tf_op jit(solution)/shard_map/reduce_scatter | solution.py:118
  10.6 3.7 copy-start.3
  12.8 220.6 %copy-start.2 = (s32[1,448]{1,0:T(1,128)S(1)}, s32[1,448]{1,0:T(1,128)}, u32[]{:S(2)}) copy-start(s32[1,448]{1,0:T(1,128)} %param.36) | copy-start | bytes 5380
  31.8 611.6 %collective-permute-start = (bf16[128,32,128]{2,0,1:T(8,128)(2,1)}, bf16[128,32,128]{2,0,1:T(8,128)(2,1)}, u32[]{:S(2)}, u32[]{:S(2)}) collective-permute-start(bf16[128,32,128]{2,0,1:T(8,128)(2,1)} %copy.98), channel_id=1, source_target_pairs={{0,4},{4,0},{8,12},{12,8},{16,20},{20,16},{24,28},{28,24},{1,5},{5... | collective-permute-start | bytes 3145736 | tf_op jit(solution)/shard_map/ppermute | solution.py:11
  233.5 202.1 %copy-start = (s32[1,448]{1,0:T(1,128)S(1)}, s32[1,448]{1,0:T(1,128)}, u32[]{:S(2)}) copy-start(s32[1,448]{1,0:T(1,128)} %param.33) | copy-start | bytes 5380
  233.5 202.1 %copy-start.1 = (s32[1,448]{1,0:T(1,128)S(1)}, s32[1,448]{1,0:T(1,128)}, u32[]{:S(2)}) copy-start(s32[1,448]{1,0:T(1,128)} %param.32) | copy-start | bytes 5380
  635.3 41.4 %copy-start.4 = (bf16[128,28,128]{2,0,1:T(8,128)(2,1)}, bf16[128,28,128]{2,0,1:T(8,128)(2,1)S(1)}, u32[]{:S(2)}) copy-start(bf16[128,28,128]{2,0,1:T(8,128)(2,1)S(1)} %get-tuple-element.1284) | copy-start | bytes 2752516
  635.3 28.4 %collective-permute-start.1 = (bf16[128,28,128]{2,0,1:T(8,128)(2,1)}, bf16[128,28,128]{2,0,1:T(8,128)(2,1)}, u32[]{:S(2)}, u32[]{:S(2)}) collective-permute-start(bf16[128,28,128]{2,0,1:T(8,128)(2,1)} %get-tuple-element.1251), channel_id=1, source_target_pairs={{0,4},{4,0},{8,12},{12,8},{16,20},{20,16},{24,28},{28,24},{1,5},{5... | collective-permute-start | bytes 2752520 | tf_op jit(solution)/shard_map/ppermute | solution.py:11
  635.9 40.8 %collective-permute-start.2 = (bf16[128,28,128]{2,0,1:T(8,128)(2,1)S(1)}, bf16[128,28,128]{2,0,1:T(8,128)(2,1)}, u32[]{:S(2)}, u32[]{:S(2)}) collective-permute-start(bf16[128,28,128]{2,0,1:T(8,128)(2,1)S(1)} %get-tuple-element.1284), channel_id=1, source_target_pairs={{0,4},{4,0},{8,12},{12,8},{16,20},{20,16},{24,28},{28,24},{1,5},{5... | collective-permute-start | bytes 2752520 | tf_op jit(solution)/shard_map/ppermute | solution.py:11
  734.2 192.1 %collective-permute-start.3 = (bf16[2,56,2,128,128]{4,3,1,2,0:T(8,128)(2,1)}, bf16[2,56,2,128,128]{4,3,1,2,0:T(8,128)(2,1)}, u32[]{:S(2)}, u32[]{:S(2)}) collective-permute-start(bf16[2,56,2,128,128]{4,3,1,2,0:T(8,128)(2,1)} %fusion.115), channel_id=1, source_target_pairs={{0,8},{4,12},{8,0},{12,4},{16,24},{20,28},{24,16},{28,20},{1,9},{5... | collective-permute-start | bytes 22020104 | tf_op jit(solution)/shard_map/ppermute | solution.py:11
  934.9 5.1 copy-start.7
  940.0 5.5 copy-start.5
  942.7 194.9 %collective-permute-start.4 = (bf16[1,56,2,128,128]{4,3,1,2,0:T(8,128)(2,1)}, bf16[1,56,2,128,128]{4,3,1,2,0:T(8,128)(2,1)}, u32[]{:S(2)}, u32[]{:S(2)}) collective-permute-start(bf16[1,56,2,128,128]{4,3,1,2,0:T(8,128)(2,1)} %dynamic-slice_convert_fusion), channel_id=1, source_target_pairs={{0,16},{4,20},{8,24},{12,28},{16,0},{20,4},{24,8},{28,12},{1,17},{... | collective-permute-start | bytes 11010056 | tf_op jit(solution)/shard_map/ppermute | solution.py:11
  954.9 3.3 copy-start.6
  967.5 3.9 copy-start.6
  980.9 3.9 copy-start.6
  994.2 3.9 copy-start.6
  1007.5 3.9 copy-start.6
  1020.9 3.9 copy-start.6
  1034.2 3.9 copy-start.6
  1047.5 3.9 copy-start.6
  1060.8 3.9 copy-start.6
  1074.2 3.9 copy-start.6
  1087.5 3.9 copy-start.6
  1100.8 3.9 copy-start.6
  1114.2 3.9 copy-start.6
  1127.5 3.9 copy-start.6
  1134.1 1.5 copy-start.8
Sparse Core Ops, SparseCore 0:
  10.1 19.4 all-gather.5
  31.8 201.6 all-gather.7
  235.7 199.8 all-gather.3
  1135.7 23.0 reduce-scatter.1
where the time goes:
time: 1170 us
  matrix products  462 us (39%)
  local copies, waits for them, and re-layouts  359 us (31%)
  waiting for transfers between devices  239 us (20%)
  other arithmetic  82.2 us (7%)
  between operations  15.4 us (1%)
    dot_general x56, matrix products, place_split(): jnp.einsum(form, rest_part, table, preferred_element_type=jnp.float32)  213 us
    all_gather x1, waiting for transfers between devices, on_device(): up_all = lax.all_gather(up_blocks, 'seq', axis=1, tiled=True)  200 us
    convert_element_type x56, local copies, waits for them, and re-layouts, place_split(): rest_part = (products - high_part.astype(jnp.float32)).astype(jnp.bfloat16)  95.1 us
    convert_element_type x56, local copies, waits for them, and re-layouts, place_split(): high_part = products.astype(jnp.bfloat16)  95 us
    dot_general x56, matrix products, place_split(): jnp.einsum(form, high_part, table, preferred_element_type=jnp.float32)  91.5 us
    dot_general x28, matrix products, return_one_group(): jnp.einsum('tsn,skn->tsk', picked, chosen, preferred_element_type=jnp.flo...  60.6 us
    dot_general x28, matrix products, project_one_group(): jnp.einsum('tsk,skn->tsn', picked, chosen, preferred_element_type=jnp.flo...  59.6 us
    gather x28, local copies, waits for them, and re-layouts, project_one_group(): picked = jnp.take(tiles, row_ids, axis=1)  55.3 us
  transfers between devices with their start and end apart: 9, of which 5 were waited for; matrix products, arithmetic and copies ran while one was open for 71% of the time, Pallas kernels for 0%

commit v1 on v0

--- a/solution.py
+++ b/solution.py
@@ -83,8 +83,13 @@
     block_size = gate_blocks.shape[2]
     row_blocks = gathered.shape[1] // block_size
     col_blocks = hidden_grad.shape[1] // block_size
-    gate_all = lax.all_gather(gate_blocks, "seq", axis=1, tiled=True)
-    up_all = lax.all_gather(up_blocks, "seq", axis=1, tiled=True)
+    gate_all, up_all = jnp.split(
+        lax.all_gather(
+            jnp.concatenate([gate_blocks, up_blocks], axis=0), "seq", axis=1, tiled=True
+        ),
+        [gate_blocks.shape[0]],
+        axis=0,
+    )
     capacity = gate_all.shape[1]
     group_size = 32
     groups = capacity // group_size

time: 1170 us -> 1560 us (1.33)
  waiting for transfers between devices: 239 us -> 599 us
  local copies, waits for them, and re-layouts: 359 us -> 380 us
    all_gather x2 -> x1, waiting for transfers between devices: 210 us -> 575 us  [on_device(): lax.all_gather(jnp.concatenate([gate_blocks, up_blocks], axis=0), 'seq',...]
    squeeze x0 -> x1, local copies, waits for them, and re-layouts: none -> 22.2 us  [on_device(): gate_all[0]]
  transfers between devices with their start and end apart: 9 -> 8, of which waited for: 5 -> 4; matrix products, arithmetic and copies ran while one was open for 71% -> 55% of each run, Pallas kernels for 0% -> 0%
where the time goes in v1:
time: 1560 us; the launch traced here: 1550 us
  waiting for transfers between devices  599 us (38%)
  matrix products  461 us (30%)
  local copies, waits for them, and re-layouts  380 us (24%)
  other arithmetic  86.4 us (6%)
    all_gather x1, waiting for transfers between devices, on_device(): lax.all_gather(jnp.concatenate([gate_blocks, up_blocks], axis=0), 'seq',...  575 us
    dot_general x56, matrix products, place_split(): jnp.einsum(form, rest_part, table, preferred_element_type=jnp.float32)  213 us
    convert_element_type x56, local copies, waits for them, and re-layouts, place_split(): high_part = products.astype(jnp.bfloat16)  94.1 us
    convert_element_type x56, local copies, waits for them, and re-layouts, place_split(): rest_part = (products - high_part.astype(jnp.float32)).astype(jnp.bfloat16)  94.1 us
    dot_general x56, matrix products, place_split(): jnp.einsum(form, high_part, table, preferred_element_type=jnp.float32)  91.2 us
    dot_general x28, matrix products, return_one_group(): jnp.einsum('tsn,skn->tsk', picked, chosen, preferred_element_type=jnp.flo...  60.6 us
    dot_general x28, matrix products, project_one_group(): jnp.einsum('tsk,skn->tsn', picked, chosen, preferred_element_type=jnp.flo...  59.5 us
    gather x28, local copies, waits for them, and re-layouts, project_one_group(): picked = jnp.take(tiles, row_ids, axis=1)  55.3 us
  transfers between devices with their start and end apart: 8, of which 4 were waited for; matrix products, arithmetic and copies ran while one was open for 55% of the time, Pallas kernels for 0%

profile of v1, /device:TPU:0, one launch (start us, length us, event | category | flops | bytes accessed | tf_op | source)
XLA Modules:
  0.0 1551.3 jit_solution(13579429911602914801)
XLA Ops:
  9.1 4.2 pad_maximum_fusion
  20.1 9.5 all-gather.5.cloned.1.call-done
  33.3 575.1 %all-gather.3.cloned.1.call-done = bf16[2,448,128,128]{3,2,1,0:T(8,128)(2,1)} async-done(((bf16[2,56,128,128]{3,2,1,0:T(8,128)(2,1)}), bf16[2,448,128,128]{3,2,1,0:T(8,128)(2,1)}) %all-gather.3.cloned.1.call-update) | async-done | bytes 29360144 | tf_op jit(solution)/shard_map/all_gather | solution.py:87
  608.4 22.2 %slice_bitcast_fusion.1 = (bf16[448,128,128]{2,1,0:T(8,128)(2,1)}, bf16[448,128,128]{2,1,0:T(8,128)(2,1)}) fusion(bf16[2,448,128,128]{3,2,1,0:T(8,128)(2,1)} %all-gather.3.cloned.1.call-done), kind=kLoop, calls=%fused_computation.125 | loop fusion | bytes 58720256 | tf_op jit(solution)/shard_map/squeeze | solution.py:100
  630.7 190.1 %while.61 = (s32[]{:T(128)}, f32[128,28,128]{2,1,0:T(8,128)}, s32[448]{0:T(512)S(1)}, s32[]{:T(128)}, bf16[448,128,128]{2,1,0:T(8,128)(2,1)}, /*index=5*/s32[448...) while((s32[]{:T(128)}, f32[128,28,128]{2,1,0:T(8,128)}, ...), condition=%wide.region_3.5_spmd.clone, body=%wide.region_2.4_spmd.clone.sunk | while | flops 196940544 | bytes 19928416 | solution.py:45
  820.8 193.0 %while.60 = (s32[]{:T(128)}, f32[128,28,128]{2,1,0:T(8,128)}, s32[448]{0:T(512)S(1)}, s32[]{:T(128)}, bf16[448,128,128]{2,1,0:T(8,128)(2,1)}, /*index=5*/s32[448...) while((s32[]{:T(128)}, f32[128,28,128]{2,1,0:T(8,128)}, ...), condition=%wide.region_1.3_spmd.clone, body=%wide.region_0.2_spmd.clone.sunk | while | flops 196940544 | bytes 19928416 | solution.py:45
  1013.8 6.5 multiply_convert_fusion.1
  1030.1 9.3 gather_fusion.5
  1039.4 9.2 gather_fusion.9
  1050.2 9.2 gather_fusion.7
  1063.8 9.1 gather_fusion.11
  1073.0 18.5 %fusion.105 = f32[224,128,128]{2,1,0:T(8,128)} fusion(bf16[224,256,128]{2,1,0:T(8,128)(2,1)} %gather_fusion.7, pred[224]{0:T(512)(128)(4,1)S(1)} %get-tuple-element.945, bf16[224,256,128]{2,1,0:T(8,128)(2,1)} %gather_fusion.5, pred[224]{0:T(512)(128)(4,1)S(1)} %get-tuple-element.947, f32[224]{0:T(256)S(1)} %get-tuple-element.944), kind=kOutput, calls=%fused_computation.143 | convolution fusion | flops 1897398272 | bytes 44041536 | tf_op jit(solution)/shard_map/tsk,tsn->skn/dot_general | solution.py:149
  1091.5 18.5 %fusion.110 = f32[224,128,128]{2,1,0:T(8,128)} fusion(bf16[224,256,128]{2,1,0:T(8,128)(2,1)} %gather_fusion.11, pred[224]{0:T(512)(128)(4,1)S(1)} %get-tuple-element.926, bf16[224,256,128]{2,1,0:T(8,128)(2,1)} %gather_fusion.9, pred[224]{0:T(512)(128)(4,1)S(1)} %get-tuple-element.923, f32[224]{0:T(256)S(1)} %get-tuple-element.943), kind=kOutput, calls=%fused_computation.144 | convolution fusion | flops 1897398272 | bytes 44041536 | tf_op jit(solution)/shard_map/tsk,tsn->skn/dot_general | solution.py:149
  1110.0 10.1 fusion.115
  1121.6 192.0 %while.62 = (s32[]{:T(128)}, f32[128,32,128]{2,1,0:T(8,128)}, s32[448]{0:T(512)S(1)}, s32[]{:T(128)}, bf16[448,128,128]{2,1,0:T(8,128)(2,1)}, /*index=5*/s32[448...) while((s32[]{:T(128)}, f32[128,32,128]{2,1,0:T(8,128)}, ...), condition=%wide.region_5.8_spmd.clone.clone, body=%wide.region_4.0_spmd.clone.clone.sunk | while | flops 205526272 | bytes 20976992 | solution.py:66
  1313.5 8.6 fusion.90
  1322.1 5.2 copy-done.7
  1332.4 185.9 %while.63 = (s32[]{:T(128)}, f32[128,32,128]{2,1,0:T(8,128)}, s32[448]{0:T(512)}, s32[]{:T(128)}, bf16[448,128,128]{2,1,0:T(8,128)(2,1)}, /*index=5*/s32[448]{0:...) while((s32[]{:T(128)}, f32[128,32,128]{2,1,0:T(8,128)}, ...), condition=%wide.region_7.10_spmd.clone.clone, body=%wide.region_6.9_spmd.clone.clone.sunk | while | flops 205526272 | bytes 24647044 | solution.py:66
  1354.5 3.9 bitcast_add_fusion.11
  1367.8 3.9 bitcast_add_fusion.11
  1381.1 3.9 bitcast_add_fusion.11
  1394.4 3.9 bitcast_add_fusion.11
  1407.8 3.9 bitcast_add_fusion.11
  1421.1 3.9 bitcast_add_fusion.11
  1434.4 3.9 bitcast_add_fusion.11
  1447.7 3.9 bitcast_add_fusion.11
  1461.1 3.9 bitcast_add_fusion.11
  1474.4 3.9 bitcast_add_fusion.11
  1487.7 3.9 bitcast_add_fusion.11
  1501.0 3.9 bitcast_add_fusion.11
  1524.5 5.9 add_bitcast_fusion
  1533.2 11.6 reduce-scatter.2.cloned.1.call-done
  (584 shorter events, 754.8 us)
Async XLA Ops:
  7.2 22.4 %all-gather.5.cloned.1.call-start = ((), (), s32[]{:S(2)}) async-start(), calls=%async_computation.2 | async-start | bytes 1310720 | tf_op jit(solution)/shard_map/all_gather | solution.py:81
  9.0 599.4 %all-gather.3.cloned.1.call-start = ((), (), s32[]{:S(2)}) async-start(), calls=%async_computation.1 | async-start | bytes 33030144 | tf_op jit(solution)/shard_map/all_gather | solution.py:87
  13.2 1.2 copy-start.9
  13.2 4.9 copy-start.3
  13.3 1531.5 %reduce-scatter.2.cloned.1.call-start = ((), (), s32[]{:S(2)}) async-start(), calls=%async_computation.3 | async-start | bytes 1310720 | tf_op jit(solution)/shard_map/reduce_scatter | solution.py:123
  31.8 598.8 %copy-start.2 = (s32[1,448]{1,0:T(1,128)S(1)}, s32[1,448]{1,0:T(1,128)}, u32[]{:S(2)}) copy-start(s32[1,448]{1,0:T(1,128)} %param.36) | copy-start | bytes 5380
  31.8 996.6 %collective-permute-start = (bf16[128,32,128]{2,0,1:T(8,128)(2,1)}, bf16[128,32,128]{2,0,1:T(8,128)(2,1)}, u32[]{:S(2)}, u32[]{:S(2)}) collective-permute-start(bf16[128,32,128]{2,0,1:T(8,128)(2,1)} %copy.68), channel_id=1, source_target_pairs={{0,4},{4,0},{8,12},{12,8},{16,20},{20,16},{24,28},{28,24},{1,5},{5... | collective-permute-start | bytes 3145736 | tf_op jit(solution)/shard_map/ppermute | solution.py:11
  630.6 190.1 %copy-start = (s32[1,448]{1,0:T(1,128)S(1)}, s32[1,448]{1,0:T(1,128)}, u32[]{:S(2)}) copy-start(s32[1,448]{1,0:T(1,128)} %param.33) | copy-start | bytes 5380
  630.7 190.1 %copy-start.1 = (s32[1,448]{1,0:T(1,128)S(1)}, s32[1,448]{1,0:T(1,128)}, u32[]{:S(2)}) copy-start(s32[1,448]{1,0:T(1,128)} %param.32) | copy-start | bytes 5380
  1020.3 42.2 %copy-start.4 = (bf16[128,28,128]{2,0,1:T(8,128)(2,1)}, bf16[128,28,128]{2,0,1:T(8,128)(2,1)S(1)}, u32[]{:S(2)}) copy-start(bf16[128,28,128]{2,0,1:T(8,128)(2,1)S(1)} %get-tuple-element.1268) | copy-start | bytes 2752516
  1020.3 28.3 %collective-permute-start.1 = (bf16[128,28,128]{2,0,1:T(8,128)(2,1)}, bf16[128,28,128]{2,0,1:T(8,128)(2,1)}, u32[]{:S(2)}, u32[]{:S(2)}) collective-permute-start(bf16[128,28,128]{2,0,1:T(8,128)(2,1)} %get-tuple-element.1235), channel_id=1, source_target_pairs={{0,4},{4,0},{8,12},{12,8},{16,20},{20,16},{24,28},{28,24},{1,5},{5... | collective-permute-start | bytes 2752520 | tf_op jit(solution)/shard_map/ppermute | solution.py:11
  1021.8 40.7 %collective-permute-start.2 = (bf16[128,28,128]{2,0,1:T(8,128)(2,1)S(1)}, bf16[128,28,128]{2,0,1:T(8,128)(2,1)}, u32[]{:S(2)}, u32[]{:S(2)}) collective-permute-start(bf16[128,28,128]{2,0,1:T(8,128)(2,1)S(1)} %get-tuple-element.1268), channel_id=1, source_target_pairs={{0,4},{4,0},{8,12},{12,8},{16,20},{20,16},{24,28},{28,24},{1,5},{5... | collective-permute-start | bytes 2752520 | tf_op jit(solution)/shard_map/ppermute | solution.py:11
  1120.0 193.5 %collective-permute-start.3 = (bf16[2,56,2,128,128]{4,3,1,2,0:T(8,128)(2,1)}, bf16[2,56,2,128,128]{4,3,1,2,0:T(8,128)(2,1)}, u32[]{:S(2)}, u32[]{:S(2)}) collective-permute-start(bf16[2,56,2,128,128]{4,3,1,2,0:T(8,128)(2,1)} %fusion.115), channel_id=1, source_target_pairs={{0,8},{4,12},{8,0},{12,4},{16,24},{20,28},{24,16},{28,20},{1,9},{5... | collective-permute-start | bytes 22020104 | tf_op jit(solution)/shard_map/ppermute | solution.py:11
  1322.1 5.2 copy-start.7
  1327.3 5.1 copy-start.5
  1330.0 194.5 %collective-permute-start.4 = (bf16[1,56,2,128,128]{4,3,1,2,0:T(8,128)(2,1)}, bf16[1,56,2,128,128]{4,3,1,2,0:T(8,128)(2,1)}, u32[]{:S(2)}, u32[]{:S(2)}) collective-permute-start(bf16[1,56,2,128,128]{4,3,1,2,0:T(8,128)(2,1)} %dynamic-slice_convert_fusion), channel_id=1, source_target_pairs={{0,16},{4,20},{8,24},{12,28},{16,0},{20,4},{24,8},{28,12},{1,17},{... | collective-permute-start | bytes 11010056 | tf_op jit(solution)/shard_map/ppermute | solution.py:11
  1341.8 3.2 copy-start.6
  1354.5 3.9 copy-start.6
  1367.8 3.9 copy-start.6
  1381.1 3.9 copy-start.6
  1394.4 3.9 copy-start.6
  1407.8 3.9 copy-start.6
  1421.1 3.9 copy-start.6
  1434.4 3.9 copy-start.6
  1447.7 3.9 copy-start.6
  1461.0 3.9 copy-start.6
  1474.4 3.9 copy-start.6
  1487.7 3.9 copy-start.6
  1501.0 3.9 copy-start.6
  1514.3 3.9 copy-start.6
  1518.3 4.3 copy-start.8
Sparse Core Ops, SparseCore 0:
  10.1 19.4 all-gather.4
  31.1 577.2 all-gather.2
  1522.7 22.0 reduce-scatter.1
